TPU v7x, 512 devices: a whole 4x8x8 slice. The times are simulated.
512 devices in a mesh: mem: 4 (over x), lat: 4 (over y_hi, core), lon: 32 (over z, y_lo).
Axes of the slice: x: 4, y: 8 (y_hi: 2, y_lo: 4; y = y_hi * 4 + y_lo), z: 8, core: 2. Of those that a mesh axis runs over, the one named last changes fastest.
Arguments:
- initial_temp: float32 [100, 128, 512], P(None, 'lon', 'lat'), may hold values from -6 to 6
- land_mask: int32 [128, 512], P('lon', 'lat'), may hold values 0 or 1
- pert_table: float32 [16, 100], replicated, may hold values from 0.03 to 0.24
- pert_index: int32 [8], P('mem'), may hold values from 0 to 15
- base_kh: float32 [100], replicated, may hold values from 0.03 to 0.24
- member_mix: bfloat16 [8, 100, 100], P('mem'), may hold values from -0.15625 to 0.15625
- base_mix: bfloat16 [100, 100], replicated, may hold values from -0.15625 to 0.15625
- owner: int32 [32768, 1], P(('lat', 'lon')), may hold values from 0 to 127; in each aligned block of 256 rows (0 to 255, 256 to 511, ...) at most 4 rows name the same one
- column: int32 [32768], P(('lat', 'lon')), may hold values from 0 to 511
- interp_w: float32 [32768, 100], P(('lat', 'lon')), may hold values from 0 to 1
- obs_inv_var: float32 [32768, 100], P(('lat', 'lon')), may hold values from 1 to 16
- observed: float32 [32768, 100], P(('lat', 'lon')), may hold values from -6 to 6
Outputs:
- member_temp: bfloat16 [8, 100, 128, 512], P('mem', None, 'lon', 'lat')
- base_temp: bfloat16 [100, 128, 512], P(None, 'lon', 'lat')
- gram_block: float32 [8, 8], replicated
- projection: float32 [8], replicated
- misfit: float32 [32768, 100], P(('lat', 'lon'))
Inputs may be any that keep to these rules, and one draw needn't show every extreme that they name: Within the records of one device no owner is named more than 4 times, and in every draw some owner is named exactly 4 times by some device's records. The column within the owner's block is the longitude offset times 128 plus the latitude offset.
All inputs are finite; a program needn't handle non-finite values. No bound on the sum of `land_mask` on one device may be relied on, other than what follows from the above.
Results may differ from a plain program's by a relative error of at most 0.012.
Values may be sent and summed in bfloat16 or wider, within the bound.
No kernel may reach another device: no remote copies, remote signals or barrier semaphores. Data moves between devices by JAX's collectives and lax.ppermute only.
A program may use at most 64 MiB of HBM per device.

v0:
```python
import jax
import jax.numpy as jnp
from jax import lax
from jax.sharding import PartitionSpec as P

STEPS = 5


def padded_2(cells, sides, width, closed):
    for axis, dim in sides:
        count = lax.axis_size(axis)
        ends = count if closed else count - 1
        head = lax.slice_in_dim(cells, 0, width, axis=dim)
        tail = lax.slice_in_dim(cells, cells.shape[dim] - width, cells.shape[dim], axis=dim)
        cells = jnp.concatenate(
            [
                lax.ppermute(tail, axis, [(i, (i + 1) % count) for i in range(ends)]),
                cells,
                lax.ppermute(head, axis, [((i + 1) % count, i) for i in range(ends)]),
            ],
            axis=dim,
        )
    return cells


def on_device(
    initial_temp,
    land_mask,
    pert_table,
    pert_index,
    base_kh,
    member_mix,
    base_mix,
    owner,
    column,
    interp_w,
    obs_inv_var,
    observed,
):
    members = pert_index.shape[0]
    levels = initial_temp.shape[0]
    width_lon = initial_temp.shape[1]
    width_lat = initial_temp.shape[2]
    table_rows = pert_table.shape[0]
    chooser = (pert_index[:, None] == jnp.arange(table_rows)[None, :]).astype(jnp.float32)
    member_kh = jnp.dot(chooser, pert_table, precision=lax.Precision.HIGHEST)
    run_kh = jnp.concatenate([member_kh, base_kh[None, :]], 0)
    run_mix = jnp.concatenate([member_mix, base_mix[None]], 0)
    run_count = members + 1
    fields = jnp.broadcast_to(
        initial_temp.astype(jnp.bfloat16)[None], (run_count, levels, width_lon, width_lat)
    )
    total_lat = width_lat * lax.axis_size("lat")
    lat_start = lax.axis_index("lat") * width_lat
    ocean_open = land_mask.astype(jnp.float32)
    for step_index in range(STEPS):
        lon_padded = padded_2(fields, (("lon", 2),), 1, True)
        padded = padded_2(lon_padded, (("lat", 3),), 1, False)
        global_rows = lat_start - (1 - 1) + jnp.arange(width_lat + 2 * (1 - 1))
        has_next = (global_rows < total_lat - 1).astype(jnp.float32)
        has_prior = (global_rows > 0).astype(jnp.float32)
        widened = padded.astype(jnp.float32)
        values = widened[:, :, 1:-1, 1:-1]
        laplace = widened[:, :, 2:, 1:-1] + widened[:, :, :-2, 1:-1] - 2.0 * values
        laplace = (
            laplace
            + has_next * (widened[:, :, 1:-1, 2:] - values)
            + has_prior * (widened[:, :, 1:-1, :-2] - values)
        )
        right_side = (values + run_kh[:, :, None, None] * laplace).astype(jnp.bfloat16)
        vertical = right_side.astype(jnp.float32) + jnp.einsum(
            "rkj,rjab->rkab", run_mix, right_side, preferred_element_type=jnp.float32
        )
        fields = (values + ocean_open * (vertical - values)).astype(jnp.bfloat16)
    owners = lax.axis_size("lat") * lax.axis_size("lon")
    prof_dev = owner.shape[0]
    capacity = max(2, 2 * prof_dev // owners)
    target = owner[:, 0]
    matches = (target[:, None] == jnp.arange(owners)[None, :]).astype(jnp.int32)
    earlier = jnp.cumsum(matches, 0) - matches
    slot_rank = jnp.sum(earlier * matches, 1)
    position = target * capacity + slot_rank
    send_ids = (
        jnp.full((owners * capacity,), -1, jnp.int32)
        .at[position]
        .set(column)
        .reshape(owners, capacity)
    )
    records = jnp.stack([interp_w, obs_inv_var, observed], 1)
    send_records = (
        jnp.zeros((owners * capacity, 3, levels), jnp.float32)
        .at[position]
        .set(records)
        .reshape(owners, capacity, 3, levels)
    )
    columns_flat = fields.reshape(run_count, levels, width_lon * width_lat)
    column_ids = lax.all_to_all(send_ids, ("lat", "lon"), split_axis=0, concat_axis=0, tiled=True)
    record_rows = lax.all_to_all(
        send_records, ("lat", "lon"), split_axis=0, concat_axis=0, tiled=True
    )
    sources = column_ids.shape[0]
    slot_count = column_ids.shape[1]
    usable = (column_ids >= 0).astype(jnp.float32).reshape(-1)
    picked = jnp.take(columns_flat, jnp.maximum(column_ids, 0).reshape(-1), axis=2).astype(
        jnp.float32
    )
    deeper = jnp.concatenate([picked[:, 1:], picked[:, -1:]], 1)
    flat_records = record_rows.reshape(sources * slot_count, 3, levels)
    weight = flat_records[:, 0].T
    inv_var = flat_records[:, 1].T * usable
    measured = flat_records[:, 2].T
    modeled = weight * picked + (1.0 - weight) * deeper
    green_cols = ((modeled[:members] - modeled[members]) * usable).astype(jnp.bfloat16)
    misfit = (measured - modeled[members]) * usable
    extras = jnp.stack([inv_var, misfit], 0)
    green_cols, extras = (
        green_cols.reshape(members, levels, sources, slot_count),
        extras.reshape(2, levels, sources, slot_count),
    )
    owner_misfit = jnp.transpose(extras[1], (1, 2, 0))
    returned = lax.all_to_all(owner_misfit, ("lat", "lon"), split_axis=0, concat_axis=0, tiled=True)
    misfit_rows = jnp.take(returned.reshape(owners * capacity, levels), position, axis=0)
    green_cols = green_cols.reshape(members, levels, -1)
    extras = extras.reshape(2, levels, -1)
    normalizer = 1.0 / (prof_dev * owners * levels)
    green_all = lax.all_gather(green_cols, "mem", axis=0, tiled=True)
    green_float = green_all.astype(jnp.float32)
    weighted = green_float * extras[0]
    gram_part = (
        jnp.einsum("mks,nks->mn", weighted, green_float, precision=lax.Precision.HIGHEST)
        * normalizer
    )
    proj_part = (
        jnp.einsum("mks,ks->m", weighted, extras[1], precision=lax.Precision.HIGHEST) * normalizer
    )
    gram_part, proj_part = (gram_part, proj_part)
    gram_block, projection = lax.psum((gram_part, proj_part), ("lat", "lon"))
    return (fields[:members], fields[members], gram_block, projection, misfit_rows)


def solution(mesh):
    placed = (
        P(None, "lon", "lat"),
        P("lon", "lat"),
        P(),
        P("mem"),
        P(),
        P("mem", None, None),
        P(),
        P(("lat", "lon"), None),
        P(("lat", "lon")),
        P(("lat", "lon"), None),
        P(("lat", "lon"), None),
        P(("lat", "lon"), None),
    )
    return jax.shard_map(
        on_device,
        mesh=mesh,
        in_specs=placed,
        out_specs=(
            P("mem", None, "lon", "lat"),
            P(None, "lon", "lat"),
            P(),
            P(),
            P(("lat", "lon"), None),
        ),
        check_vma=False,
    )
```

profile of v0, /device:TPU:258, one launch (start us, length us, event | category | flops | bytes accessed | tf_op | source)
XLA Modules:
  0.0 559.3 jit_solution(4841442048766482967)
XLA Ops:
  0.6 1.0 copy.80
  1.6 4.6 collective-permute-start.1
  6.3 1.9 collective-permute-start
  8.2 0.8 copy.43
  9.3 0.8 fusion.125
  10.1 0.7 pad_maximum_fusion.6
  10.8 5.7 %collective-permute-done = bf16[3,100,1,128]{3,1,2,0:T(8,128)(2,1)S(1)} collective-permute-done((bf16[3,100,1,128]{3,1,2,0:T(8,128)(2,1)S(1)}, bf16[3,100,1,128]{3,1,2,0:T(8,128)(2,1)S(1)}, u32[]{:S(2)}, u32[]{:S(2)}) %collective-permute-start) | collective-permute-done | bytes 76832 | tf_op jit(solution)/shard_map/ppermute | solution.py:17
  16.8 1.3 collective-permute-start.2
  18.1 1.3 collective-permute-start.3
  19.6 5.7 %collective-permute-done.3 = bf16[3,100,6,1]{3,1,2,0:T(8,128)(2,1)S(1)} collective-permute-done((bf16[3,100,6,1]{3,1,2,0:T(8,128)(2,1)S(1)}, bf16[3,100,6,1]{3,1,2,0:T(8,128)(2,1)S(1)}, u32[]{:S(2)}, u32[]{:S(2)}) %collective-permute-start.3) | collective-permute-done | bytes 3632 | tf_op jit(solution)/shard_map/ppermute | solution.py:19
  25.8 1.6 fusion.19
  27.4 1.9 collective-permute-start.4
  29.4 7.8 %collective-permute-start.5 = (bf16[3,100,1,128]{3,1,2,0:T(8,128)(2,1)S(1)}, bf16[3,100,1,128]{3,1,2,0:T(8,128)(2,1)S(1)}, u32[]{:S(2)}, u32[]{:S(2)}) collective-permute-start(bf16[3,100,1,128]{3,1,2,0:T(8,128)(2,1)S(1)} %get-tuple-element.41), channel_id=1, source_target_pairs={{1,0},{2,1},{3,2},{4,3},{5,4},{6,5},{7,6},{8,7},{9,8},{10,9},{11,1... | collective-permute-start | bytes 230408 | tf_op jit(solution)/shard_map/ppermute | solution.py:19
  37.7 1.6 collective-permute-done.5
  39.5 13.3 %collective-permute-start.6 = (bf16[3,100,6,1]{3,1,2,0:T(8,128)(2,1)S(1)}, bf16[3,100,6,1]{3,1,2,0:T(8,128)(2,1)S(1)}, u32[]{:S(2)}, u32[]{:S(2)}) collective-permute-start(bf16[3,100,6,1]{3,1,2,0:T(8,128)(2,1)S(1)} %get-tuple-element.30), channel_id=1, source_target_pairs={{0,32},{32,64},{64,96},{1,33},{33,65},{65,97},{2,34},{34,66},{66,9... | collective-permute-start | bytes 10808 | tf_op jit(solution)/shard_map/ppermute | solution.py:17
  52.8 1.3 collective-permute-start.7
  54.1 1.6 scatter_custom_fusion.1
  55.7 0.7 all_to_all.13
  56.4 18.1 %all-to-all-start.1 = ((s32[128,1,4]{2,1,0:T(1,128)}), s32[128,1,4]{2,1,0:T(1,128)S(1)}, u32[]{:S(2)}, u32[]{:S(2)}) async-start(s32[128,1,4]{2,1,0:T(1,128)} %bitcast.22), calls=%async_computation.1 | async-start | bytes 131072 | tf_op jit(solution)/shard_map/all_to_all | solution.py:97
  75.2 1.6 fusion.20
  76.8 3.4 collective-permute-start.8
  80.2 6.4 %collective-permute-start.9 = (bf16[3,100,1,128]{3,1,2,0:T(8,128)(2,1)S(1)}, bf16[3,100,1,128]{3,1,2,0:T(8,128)(2,1)S(1)}, u32[]{:S(2)}, u32[]{:S(2)}) collective-permute-start(bf16[3,100,1,128]{3,1,2,0:T(8,128)(2,1)S(1)} %get-tuple-element.39), channel_id=1, source_target_pairs={{1,0},{2,1},{3,2},{4,3},{5,4},{6,5},{7,6},{8,7},{9,8},{10,9},{11,1... | collective-permute-start | bytes 230408 | tf_op jit(solution)/shard_map/ppermute | solution.py:19
  86.6 0.7 collective-permute-done.8
  87.3 1.3 collective-permute-done.9
  88.6 1.1 fusion.138
  89.8 1.3 collective-permute-start.10
  91.1 1.5 collective-permute-start.11
  93.0 7.1 %scatter_fusion = f32[512,3,100]{2,1,0:T(4,128)S(1)} fusion(f32[512,3,100]{2,1,0:T(4,128)S(1)} %broadcast_in_dim.33, s32[256]{0:T(256)S(1)} %bitcast.104, f32[256,3,100]{2,1,0:T(4,128)S(1)} %copy.45), kind=kCustom, calls=%fused_computation.2 | custom fusion | bytes 922624 | tf_op jit(solution)/shard_map/scatter | solution.py:93
  100.0 1.1 copy.47
  101.7 1.6 fusion.21
  103.3 1.9 collective-permute-start.12
  105.2 8.2 %collective-permute-start.13 = (bf16[3,100,1,128]{3,1,2,0:T(8,128)(2,1)S(1)}, bf16[3,100,1,128]{3,1,2,0:T(8,128)(2,1)S(1)}, u32[]{:S(2)}, u32[]{:S(2)}) collective-permute-start(bf16[3,100,1,128]{3,1,2,0:T(8,128)(2,1)S(1)} %get-tuple-element.37), channel_id=1, source_target_pairs={{1,0},{2,1},{3,2},{4,3},{5,4},{6,5},{7,6},{8,7},{9,8},{10,9},{11,1... | collective-permute-start | bytes 230408 | tf_op jit(solution)/shard_map/ppermute | solution.py:19
  113.4 21.5 %all-to-all-start = ((f32[128,4,3,100]{3,1,2,0:T(4,128)}), f32[128,4,3,100]{3,1,2,0:T(4,128)S(1)}, u32[]{:S(2)}, u32[]{:S(2)}) async-start(f32[128,4,3,100]{3,1,2,0:T(4,128)} %copy.47), calls=%async_computation | async-start | bytes 1572864 | tf_op jit(solution)/shard_map/all_to_all | solution.py:98
  135.5 2.3 collective-permute-start.14
  137.8 1.3 collective-permute-start.15
  139.4 0.8 copy-done.4
  140.1 6.5 %collective-permute-done.15 = bf16[3,100,6,1]{3,1,2,0:T(8,128)(2,1)} collective-permute-done((bf16[3,100,6,1]{3,1,2,0:T(8,128)(2,1)S(1)}, bf16[3,100,6,1]{3,1,2,0:T(8,128)(2,1)}, u32[]{:S(2)}, u32[]{:S(2)}) %collective-permute-start.15) | collective-permute-done | bytes 3632 | tf_op jit(solution)/shard_map/ppermute | solution.py:19
  146.7 1.7 maximum_convert_fusion.3
  148.4 1.6 fusion.22
  150.0 2.5 collective-permute-start.16
  152.5 7.3 %collective-permute-start.17 = (bf16[3,100,1,128]{3,1,2,0:T(8,128)(2,1)S(1)}, bf16[3,100,1,128]{3,1,2,0:T(8,128)(2,1)S(1)}, u32[]{:S(2)}, u32[]{:S(2)}) collective-permute-start(bf16[3,100,1,128]{3,1,2,0:T(8,128)(2,1)S(1)} %get-tuple-element.35), channel_id=1, source_target_pairs={{1,0},{2,1},{3,2},{4,3},{5,4},{6,5},{7,6},{8,7},{9,8},{10,9},{11,1... | collective-permute-start | bytes 230408 | tf_op jit(solution)/shard_map/ppermute | solution.py:19
  160.0 1.6 collective-permute-done.16
  162.1 23.8 %collective-permute-start.18 = (bf16[3,100,6,1]{3,1,2,0:T(8,128)(2,1)S(1)}, bf16[3,100,6,1]{3,1,2,0:T(8,128)(2,1)S(1)}, u32[]{:S(2)}, u32[]{:S(2)}) collective-permute-start(bf16[3,100,6,1]{3,1,2,0:T(8,128)(2,1)S(1)} %get-tuple-element.24), channel_id=1, source_target_pairs={{0,32},{32,64},{64,96},{1,33},{33,65},{65,97},{2,34},{34,66},{66,9... | collective-permute-start | bytes 10808 | tf_op jit(solution)/shard_map/ppermute | solution.py:17
  186.0 1.5 collective-permute-start.19
  187.8 0.8 copy-done.3
  188.5 1.7 collective-permute-done.19
  190.2 1.7 maximum_convert_fusion.4
  192.0 1.6 fusion.23
  194.3 2.1 gather_fusion
  196.4 1.8 convert_bitcast_fusion
  198.8 0.6 slice.289
  199.4 0.7 copy.57
  200.1 0.8 copy.56
  201.2 1.9 fusion.36
  203.4 1.5 fusion.94
  204.9 0.8 fusion.116
  206.1 24.3 %all-to-all-start.2 = ((f32[128,4,100]{2,1,0:T(4,128)}), f32[128,4,100]{2,1,0:T(4,128)S(1)}, u32[]{:S(2)}, u32[]{:S(2)}) async-start(f32[128,4,100]{2,1,0:T(4,128)} %bitcast.35), calls=%async_computation.2 | async-start | bytes 524288 | tf_op jit(solution)/shard_map/all_to_all | solution.py:121
  230.4 1.1 copy.60
  231.5 14.8 %all_gather.3 = bf16[8,100,512]{2,1,0:T(8,128)(2,1)S(1)} all-gather(bf16[2,100,512]{2,1,0:T(8,128)(2,1)S(1)} %copy.52), channel_id=1, replica_groups=mesh['mem'=4,'lat'=4,'lon'=32] {'mem'}, dimensions={0}, use_global_device_ids=true | all-gather | bytes 1024000 | tf_op jit(solution)/shard_map/all_gather | solution.py:126
  246.6 3.9 fusion.33
  250.4 2.6 fusion.27
  253.0 304.7 %all-reduce = (f32[8,8]{1,0:T(8,128)}, f32[8]{0:T(128)}) all-reduce(f32[8,8]{1,0:T(8,128)S(1)} %fusion.27, f32[8]{0:T(128)S(1)} %fusion.33), channel_id=1, replica_groups=mesh['mem'=4,'lat'=4,'lon'=32] {'lat','lon'}, use_global_device_ids=true, to_apply=%region_5.6 | all-reduce | flops 72 | bytes 576 | tf_op jit(solution)/shard_map/psum | solution.py:137
  557.8 0.7 gather_fusion.1
  558.6 0.7 copy.58
  (94 shorter events, 8.1 us)
Async XLA Ops:
  0.6 8.6 %copy-start = (f32[16,100]{1,0:T(8,128)S(1)}, f32[16,100]{1,0:T(8,128)}, u32[]{:S(2)}) copy-start(f32[16,100]{1,0:T(8,128)} %param.14) | copy-start | bytes 19204
  1.6 9.2 %collective-permute-start.1 = (bf16[3,100,1,128]{3,1,2,0:T(8,128)(2,1)S(1)}, bf16[3,100,1,128]{3,1,2,0:T(8,128)(2,1)S(1)}, u32[]{:S(2)}, u32[]{:S(2)}) collective-permute-start(bf16[3,100,1,128]{3,1,2,0:T(8,128)(2,1)S(1)} %broadcast_in_dim.30), channel_id=1, source_target_pairs={{1,0},{2,1},{3,2},{4,3},{5,4},{6,5},{7,6},{8,7},{9,8},{10,9},{11,1... | collective-permute-start | bytes 230408 | tf_op jit(solution)/shard_map/ppermute | solution.py:19
  6.3 10.2 %collective-permute-start = (bf16[3,100,1,128]{3,1,2,0:T(8,128)(2,1)S(1)}, bf16[3,100,1,128]{3,1,2,0:T(8,128)(2,1)S(1)}, u32[]{:S(2)}, u32[]{:S(2)}) collective-permute-start(bf16[3,100,1,128]{3,1,2,0:T(8,128)(2,1)S(1)} %broadcast_in_dim.28), channel_id=1, source_target_pairs={{0,1},{1,2},{2,3},{3,4},{4,5},{5,6},{6,7},{7,8},{8,9},{9,10},{10,1... | collective-permute-start | bytes 230408 | tf_op jit(solution)/shard_map/ppermute | solution.py:17
  9.0 10.5 %copy-start.10 = (s32[4,128]{1,0:T(4,128)S(1)}, s32[4,128]{1,0:T(4,128)}, u32[]{:S(2)}) copy-start(s32[4,128]{1,0:T(4,128)} %param.13) | copy-start | bytes 6148
  9.0 10.5 %copy-start.8 = (bf16[2,100,100]{2,0,1:T(2,128)(2,1)S(1)}, bf16[2,100,100]{2,0,1:T(2,128)(2,1)}, u32[]{:S(2)}) copy-start(bf16[2,100,100]{2,0,1:T(2,128)(2,1)} %param.17) | copy-start | bytes 120004
  16.8 9.0 %copy-start.11 = (bf16[100,100]{1,0:T(8,128)(2,1)S(1)}, bf16[100,100]{1,0:T(8,128)(2,1)}, u32[]{:S(2)}) copy-start(bf16[100,100]{1,0:T(8,128)(2,1)} %param.18) | copy-start | bytes 60004
  16.8 2.8 collective-permute-start.2
  18.1 7.1 %collective-permute-start.3 = (bf16[3,100,6,1]{3,1,2,0:T(8,128)(2,1)S(1)}, bf16[3,100,6,1]{3,1,2,0:T(8,128)(2,1)S(1)}, u32[]{:S(2)}, u32[]{:S(2)}) collective-permute-start(bf16[3,100,6,1]{3,1,2,0:T(8,128)(2,1)S(1)} %get-tuple-element.33), channel_id=1, source_target_pairs={{32,0},{64,32},{96,64},{33,1},{65,33},{97,65},{34,2},{66,34},{98,6... | collective-permute-start | bytes 10808 | tf_op jit(solution)/shard_map/ppermute | solution.py:19
  25.8 11.4 %copy-start.9 = (s32[256,1]{0,1:T(1,128)S(1)}, s32[256,1]{0,1:T(1,128)}, u32[]{:S(2)}) copy-start(s32[256,1]{0,1:T(1,128)} %param.19) | copy-start | bytes 3076
  27.4 10.2 %collective-permute-start.4 = (bf16[3,100,1,128]{3,1,2,0:T(8,128)(2,1)S(1)}, bf16[3,100,1,128]{3,1,2,0:T(8,128)(2,1)S(1)}, u32[]{:S(2)}, u32[]{:S(2)}) collective-permute-start(bf16[3,100,1,128]{3,1,2,0:T(8,128)(2,1)S(1)} %get-tuple-element.40), channel_id=1, source_target_pairs={{0,1},{1,2},{2,3},{3,4},{4,5},{5,6},{6,7},{7,8},{8,9},{9,10},{10,1... | collective-permute-start | bytes 230408 | tf_op jit(solution)/shard_map/ppermute | solution.py:17
  29.4 9.9 %collective-permute-start.5 = (bf16[3,100,1,128]{3,1,2,0:T(8,128)(2,1)S(1)}, bf16[3,100,1,128]{3,1,2,0:T(8,128)(2,1)S(1)}, u32[]{:S(2)}, u32[]{:S(2)}) collective-permute-start(bf16[3,100,1,128]{3,1,2,0:T(8,128)(2,1)S(1)} %get-tuple-element.41), channel_id=1, source_target_pairs={{1,0},{2,1},{3,2},{4,3},{5,4},{6,5},{7,6},{8,7},{9,8},{10,9},{11,1... | collective-permute-start | bytes 230408 | tf_op jit(solution)/shard_map/ppermute | solution.py:19
  39.5 35.1 %collective-permute-start.6 = (bf16[3,100,6,1]{3,1,2,0:T(8,128)(2,1)S(1)}, bf16[3,100,6,1]{3,1,2,0:T(8,128)(2,1)S(1)}, u32[]{:S(2)}, u32[]{:S(2)}) collective-permute-start(bf16[3,100,6,1]{3,1,2,0:T(8,128)(2,1)S(1)} %get-tuple-element.30), channel_id=1, source_target_pairs={{0,32},{32,64},{64,96},{1,33},{33,65},{65,97},{2,34},{34,66},{66,9... | collective-permute-start | bytes 10808 | tf_op jit(solution)/shard_map/ppermute | solution.py:17
  52.8 21.8 %collective-permute-start.7 = (bf16[3,100,6,1]{3,1,2,0:T(8,128)(2,1)S(1)}, bf16[3,100,6,1]{3,1,2,0:T(8,128)(2,1)S(1)}, u32[]{:S(2)}, u32[]{:S(2)}) collective-permute-start(bf16[3,100,6,1]{3,1,2,0:T(8,128)(2,1)S(1)} %get-tuple-element.31), channel_id=1, source_target_pairs={{32,0},{64,32},{96,64},{33,1},{65,33},{97,65},{34,2},{66,34},{98,6... | collective-permute-start | bytes 10808 | tf_op jit(solution)/shard_map/ppermute | solution.py:19
  56.4 57.0 %all-to-all-start.1 = ((s32[128,1,4]{2,1,0:T(1,128)}), s32[128,1,4]{2,1,0:T(1,128)S(1)}, u32[]{:S(2)}, u32[]{:S(2)}) async-start(s32[128,1,4]{2,1,0:T(1,128)} %bitcast.22), calls=%async_computation.1 | async-start | bytes 131072 | tf_op jit(solution)/shard_map/all_to_all | solution.py:97
  75.1 11.4 %copy-start.5 = (f32[256,100]{0,1:T(8,128)S(1)}, f32[256,100]{0,1:T(8,128)}, u32[]{:S(2)}) copy-start(f32[256,100]{0,1:T(8,128)} %param.23) | copy-start | bytes 307204
  75.1 11.4 %copy-start.6 = (f32[256,100]{0,1:T(8,128)S(1)}, f32[256,100]{0,1:T(8,128)}, u32[]{:S(2)}) copy-start(f32[256,100]{0,1:T(8,128)} %param.22) | copy-start | bytes 307204
  75.1 11.4 %copy-start.7 = (f32[256,100]{0,1:T(8,128)S(1)}, f32[256,100]{0,1:T(8,128)}, u32[]{:S(2)}) copy-start(f32[256,100]{0,1:T(8,128)} %param.21) | copy-start | bytes 307204
  76.8 10.5 %collective-permute-start.8 = (bf16[3,100,1,128]{3,1,2,0:T(8,128)(2,1)S(1)}, bf16[3,100,1,128]{3,1,2,0:T(8,128)(2,1)S(1)}, u32[]{:S(2)}, u32[]{:S(2)}) collective-permute-start(bf16[3,100,1,128]{3,1,2,0:T(8,128)(2,1)S(1)} %get-tuple-element.38), channel_id=1, source_target_pairs={{0,1},{1,2},{2,3},{3,4},{4,5},{5,6},{6,7},{7,8},{8,9},{9,10},{10,1... | collective-permute-start | bytes 230408 | tf_op jit(solution)/shard_map/ppermute | solution.py:17
  80.2 8.4 %collective-permute-start.9 = (bf16[3,100,1,128]{3,1,2,0:T(8,128)(2,1)S(1)}, bf16[3,100,1,128]{3,1,2,0:T(8,128)(2,1)S(1)}, u32[]{:S(2)}, u32[]{:S(2)}) collective-permute-start(bf16[3,100,1,128]{3,1,2,0:T(8,128)(2,1)S(1)} %get-tuple-element.39), channel_id=1, source_target_pairs={{1,0},{2,1},{3,2},{4,3},{5,4},{6,5},{7,6},{8,7},{9,8},{10,9},{11,1... | collective-permute-start | bytes 230408 | tf_op jit(solution)/shard_map/ppermute | solution.py:19
  89.8 11.4 %collective-permute-start.10 = (bf16[3,100,6,1]{3,1,2,0:T(8,128)(2,1)}, bf16[3,100,6,1]{3,1,2,0:T(8,128)(2,1)S(1)}, u32[]{:S(2)}, u32[]{:S(2)}) collective-permute-start(bf16[3,100,6,1]{3,1,2,0:T(8,128)(2,1)} %get-tuple-element.28), channel_id=1, source_target_pairs={{0,32},{32,64},{64,96},{1,33},{33,65},{65,97},{2,34},{34,66},{66,9... | collective-permute-start | bytes 10808 | tf_op jit(solution)/shard_map/ppermute | solution.py:17
  91.1 10.1 %collective-permute-start.11 = (bf16[3,100,6,1]{3,1,2,0:T(8,128)(2,1)}, bf16[3,100,6,1]{3,1,2,0:T(8,128)(2,1)S(1)}, u32[]{:S(2)}, u32[]{:S(2)}) collective-permute-start(bf16[3,100,6,1]{3,1,2,0:T(8,128)(2,1)} %get-tuple-element.29), channel_id=1, source_target_pairs={{32,0},{64,32},{96,64},{33,1},{65,33},{97,65},{34,2},{66,34},{98,6... | collective-permute-start | bytes 10808 | tf_op jit(solution)/shard_map/ppermute | solution.py:19
  103.3 31.9 %collective-permute-start.12 = (bf16[3,100,1,128]{3,1,2,0:T(8,128)(2,1)S(1)}, bf16[3,100,1,128]{3,1,2,0:T(8,128)(2,1)S(1)}, u32[]{:S(2)}, u32[]{:S(2)}) collective-permute-start(bf16[3,100,1,128]{3,1,2,0:T(8,128)(2,1)S(1)} %get-tuple-element.36), channel_id=1, source_target_pairs={{0,1},{1,2},{2,3},{3,4},{4,5},{5,6},{6,7},{7,8},{8,9},{9,10},{10,1... | collective-permute-start | bytes 230408 | tf_op jit(solution)/shard_map/ppermute | solution.py:17
  105.2 30.0 %collective-permute-start.13 = (bf16[3,100,1,128]{3,1,2,0:T(8,128)(2,1)S(1)}, bf16[3,100,1,128]{3,1,2,0:T(8,128)(2,1)S(1)}, u32[]{:S(2)}, u32[]{:S(2)}) collective-permute-start(bf16[3,100,1,128]{3,1,2,0:T(8,128)(2,1)S(1)} %get-tuple-element.37), channel_id=1, source_target_pairs={{1,0},{2,1},{3,2},{4,3},{5,4},{6,5},{7,6},{8,7},{9,8},{10,9},{11,1... | collective-permute-start | bytes 230408 | tf_op jit(solution)/shard_map/ppermute | solution.py:19
  113.4 87.4 %all-to-all-start = ((f32[128,4,3,100]{3,1,2,0:T(4,128)}), f32[128,4,3,100]{3,1,2,0:T(4,128)S(1)}, u32[]{:S(2)}, u32[]{:S(2)}) async-start(f32[128,4,3,100]{3,1,2,0:T(4,128)} %copy.47), calls=%async_computation | async-start | bytes 1572864 | tf_op jit(solution)/shard_map/all_to_all | solution.py:98
  135.5 3.9 collective-permute-start.14
  137.8 8.9 %collective-permute-start.15 = (bf16[3,100,6,1]{3,1,2,0:T(8,128)(2,1)S(1)}, bf16[3,100,6,1]{3,1,2,0:T(8,128)(2,1)}, u32[]{:S(2)}, u32[]{:S(2)}) collective-permute-start(bf16[3,100,6,1]{3,1,2,0:T(8,128)(2,1)S(1)} %get-tuple-element.27), channel_id=1, source_target_pairs={{32,0},{64,32},{96,64},{33,1},{65,33},{97,65},{34,2},{66,34},{98,6... | collective-permute-start | bytes 10808 | tf_op jit(solution)/shard_map/ppermute | solution.py:19
  139.4 0.8 copy-start.4
  150.0 11.6 %collective-permute-start.16 = (bf16[3,100,1,128]{3,1,2,0:T(8,128)(2,1)S(1)}, bf16[3,100,1,128]{3,1,2,0:T(8,128)(2,1)S(1)}, u32[]{:S(2)}, u32[]{:S(2)}) collective-permute-start(bf16[3,100,1,128]{3,1,2,0:T(8,128)(2,1)S(1)} %get-tuple-element.34), channel_id=1, source_target_pairs={{0,1},{1,2},{2,3},{3,4},{4,5},{5,6},{6,7},{7,8},{8,9},{9,10},{10,1... | collective-permute-start | bytes 230408 | tf_op jit(solution)/shard_map/ppermute | solution.py:17
  152.5 9.4 %collective-permute-start.17 = (bf16[3,100,1,128]{3,1,2,0:T(8,128)(2,1)S(1)}, bf16[3,100,1,128]{3,1,2,0:T(8,128)(2,1)S(1)}, u32[]{:S(2)}, u32[]{:S(2)}) collective-permute-start(bf16[3,100,1,128]{3,1,2,0:T(8,128)(2,1)S(1)} %get-tuple-element.35), channel_id=1, source_target_pairs={{1,0},{2,1},{3,2},{4,3},{5,4},{6,5},{7,6},{8,7},{9,8},{10,9},{11,1... | collective-permute-start | bytes 230408 | tf_op jit(solution)/shard_map/ppermute | solution.py:19
  162.1 25.6 %collective-permute-start.18 = (bf16[3,100,6,1]{3,1,2,0:T(8,128)(2,1)S(1)}, bf16[3,100,6,1]{3,1,2,0:T(8,128)(2,1)S(1)}, u32[]{:S(2)}, u32[]{:S(2)}) collective-permute-start(bf16[3,100,6,1]{3,1,2,0:T(8,128)(2,1)S(1)} %get-tuple-element.24), channel_id=1, source_target_pairs={{0,32},{32,64},{64,96},{1,33},{33,65},{65,97},{2,34},{34,66},{66,9... | collective-permute-start | bytes 10808 | tf_op jit(solution)/shard_map/ppermute | solution.py:17
  186.0 4.2 collective-permute-start.19
  187.8 0.8 copy-start.3
  193.5 0.7 copy-start.1
  198.1 1.2 copy-start.2
  198.1 1.9 slice-start
  206.1 351.7 %all-to-all-start.2 = ((f32[128,4,100]{2,1,0:T(4,128)}), f32[128,4,100]{2,1,0:T(4,128)S(1)}, u32[]{:S(2)}, u32[]{:S(2)}) async-start(f32[128,4,100]{2,1,0:T(4,128)} %bitcast.35), calls=%async_computation.2 | async-start | bytes 524288 | tf_op jit(solution)/shard_map/all_to_all | solution.py:121
where the time goes:
time: 560 us; the launch traced here: 559 us
  blocking collectives  320 us (57%)
  starting transfers between devices  159 us (28%)
  local copies, waits for them, and re-layouts  25.4 us (5%)
  waiting for transfers between devices  25.4 us (5%)
  matrix products  15.2 us (3%)
  other arithmetic  13.8 us (2%)
    psum x1, blocking collectives, on_device(): gram_block, projection = lax.psum((gram_part, proj_part), ('lat', 'lon'))  305 us
    ppermute x10, starting transfers between devices, padded_2(): lax.ppermute(tail, axis, [(i, (i + 1) % count) for i in range(ends)])  53.6 us
    ppermute x10, starting transfers between devices, padded_2(): lax.ppermute(head, axis, [((i + 1) % count, i) for i in range(ends)])  41.1 us
    all_to_all x1, starting transfers between devices, on_device(): lax.all_to_all(owner_misfit, ('lat', 'lon'), split_axis=0, concat_axis=0,...  24.3 us
    all_to_all x1, starting transfers between devices, on_device(): lax.all_to_all(send_records, ('lat', 'lon'), split_axis=0, concat_axis=0,...  21.5 us
    all_to_all x1, starting transfers between devices, on_device(): lax.all_to_all(send_ids, ('lat', 'lon'), split_axis=0, concat_axis=0, til...  18.1 us
    ppermute x10, waiting for transfers between devices, padded_2(): lax.ppermute(head, axis, [((i + 1) % count, i) for i in range(ends)])  17.1 us
    all_gather x1, blocking collectives, on_device(): green_all = lax.all_gather(green_cols, 'mem', axis=0, tiled=True)  14.8 us
  transfers between devices with their start and end apart: 23, of which 10 were waited for; matrix products, arithmetic and copies ran while one was open for 7% of the time, Pallas kernels for 0%

commit v1 on v0

--- a/solution.py
+++ b/solution.py
@@ -4,6 +4,10 @@
 from jax.sharding import PartitionSpec as P
 
 STEPS = 5
+
+
+def push_the_kinds(here_x, shard_axis, ax_name="lat"):
+    return lax.psum(lax.psum(here_x, shard_axis), ax_name)
 
 
 def padded_2(cells, sides, width, closed):
@@ -134,7 +138,7 @@
         jnp.einsum("mks,ks->m", weighted, extras[1], precision=lax.Precision.HIGHEST) * normalizer
     )
     gram_part, proj_part = (gram_part, proj_part)
-    gram_block, projection = lax.psum((gram_part, proj_part), ("lat", "lon"))
+    gram_block, projection = push_the_kinds((gram_part, proj_part), "lon")
     return (fields[:members], fields[members], gram_block, projection, misfit_rows)
 
 

time: 560 us -> 352 us (0.63)
  the two profiles are of different devices: /device:TPU:258 before, /device:TPU:1 now
where the time goes in v1:
time: 352 us; the launch traced here: 351 us
  starting transfers between devices  123 us (35%)
  blocking collectives  106 us (30%)
  waiting for transfers between devices  65.5 us (19%)
  local copies, waits for them, and re-layouts  25.4 us (7%)
  matrix products  15.2 us (4%)
  other arithmetic  13.8 us (4%)
    psum x2, blocking collectives, push_the_kinds(): return lax.psum(lax.psum(here_x, shard_axis), ax_name)  93.4 us
    ppermute x10, starting transfers between devices, padded_2(): lax.ppermute(head, axis, [((i + 1) % count, i) for i in range(ends)])  51.4 us
    ppermute x10, starting transfers between devices, padded_2(): lax.ppermute(tail, axis, [(i, (i + 1) % count) for i in range(ends)])  40.7 us
    ppermute x10, waiting for transfers between devices, padded_2(): lax.ppermute(head, axis, [((i + 1) % count, i) for i in range(ends)])  40.1 us
    ppermute x10, waiting for transfers between devices, padded_2(): lax.ppermute(tail, axis, [(i, (i + 1) % count) for i in range(ends)])  25.4 us
    all_gather x1, blocking collectives, on_device(): green_all = lax.all_gather(green_cols, 'mem', axis=0, tiled=True)  12.9 us
    all_to_all x1, starting transfers between devices, on_device(): lax.all_to_all(send_ids, ('lat', 'lon'), split_axis=0, concat_axis=0, til...  12 us
    all_to_all x1, starting transfers between devices, on_device(): lax.all_to_all(owner_misfit, ('lat', 'lon'), split_axis=0, concat_axis=0,...  10.7 us
  transfers between devices with their start and end apart: 23, of which 12 were waited for; matrix products, arithmetic and copies ran while one was open for 12% of the time, Pallas kernels for 0%

profile of v1, /device:TPU:1, one launch (start us, length us, event | category | flops | bytes accessed | tf_op | source)
XLA Modules:
  0.0 350.8 jit_solution(720471360907943509)
XLA Ops:
  0.6 1.0 copy.80
  1.6 14.5 %collective-permute-start.1 = (bf16[3,100,1,128]{3,1,2,0:T(8,128)(2,1)S(1)}, bf16[3,100,1,128]{3,1,2,0:T(8,128)(2,1)S(1)}, u32[]{:S(2)}, u32[]{:S(2)}) collective-permute-start(bf16[3,100,1,128]{3,1,2,0:T(8,128)(2,1)S(1)} %broadcast_in_dim.30), channel_id=1, source_target_pairs={{1,0},{2,1},{3,2},{4,3},{5,4},{6,5},{7,6},{8,7},{9,8},{10,9},{11,1... | collective-permute-start | bytes 230408 | tf_op jit(solution)/shard_map/ppermute | solution.py:23
  16.2 1.9 collective-permute-start
  18.1 0.8 copy.43
  19.2 0.8 fusion.125
  20.7 4.5 %collective-permute-done = bf16[3,100,1,128]{3,1,2,0:T(8,128)(2,1)S(1)} collective-permute-done((bf16[3,100,1,128]{3,1,2,0:T(8,128)(2,1)S(1)}, bf16[3,100,1,128]{3,1,2,0:T(8,128)(2,1)S(1)}, u32[]{:S(2)}, u32[]{:S(2)}) %collective-permute-start) | collective-permute-done | bytes 76832 | tf_op jit(solution)/shard_map/ppermute | solution.py:21
  25.6 6.7 %collective-permute-start.2 = (bf16[3,100,6,1]{3,1,2,0:T(8,128)(2,1)S(1)}, bf16[3,100,6,1]{3,1,2,0:T(8,128)(2,1)S(1)}, u32[]{:S(2)}, u32[]{:S(2)}) collective-permute-start(bf16[3,100,6,1]{3,1,2,0:T(8,128)(2,1)S(1)} %get-tuple-element.34), channel_id=1, source_target_pairs={{0,32},{32,64},{64,96},{1,33},{33,65},{65,97},{2,34},{34,66},{66,9... | collective-permute-start | bytes 10808 | tf_op jit(solution)/shard_map/ppermute | solution.py:21
  32.3 1.9 collective-permute-start.3
  34.3 3.7 %collective-permute-done.2 = bf16[3,100,6,1]{3,1,2,0:T(8,128)(2,1)S(1)} collective-permute-done((bf16[3,100,6,1]{3,1,2,0:T(8,128)(2,1)S(1)}, bf16[3,100,6,1]{3,1,2,0:T(8,128)(2,1)S(1)}, u32[]{:S(2)}, u32[]{:S(2)}) %collective-permute-start.2) | collective-permute-done | bytes 3632 | tf_op jit(solution)/shard_map/ppermute | solution.py:21
  38.1 8.8 %collective-permute-done.3 = bf16[3,100,6,1]{3,1,2,0:T(8,128)(2,1)S(1)} collective-permute-done((bf16[3,100,6,1]{3,1,2,0:T(8,128)(2,1)S(1)}, bf16[3,100,6,1]{3,1,2,0:T(8,128)(2,1)S(1)}, u32[]{:S(2)}, u32[]{:S(2)}) %collective-permute-start.3) | collective-permute-done | bytes 3632 | tf_op jit(solution)/shard_map/ppermute | solution.py:23
  47.5 1.6 fusion.19
  49.1 1.9 collective-permute-start.4
  51.0 7.3 %collective-permute-start.5 = (bf16[3,100,1,128]{3,1,2,0:T(8,128)(2,1)S(1)}, bf16[3,100,1,128]{3,1,2,0:T(8,128)(2,1)S(1)}, u32[]{:S(2)}, u32[]{:S(2)}) collective-permute-start(bf16[3,100,1,128]{3,1,2,0:T(8,128)(2,1)S(1)} %get-tuple-element.43), channel_id=1, source_target_pairs={{1,0},{2,1},{3,2},{4,3},{5,4},{6,5},{7,6},{8,7},{9,8},{10,9},{11,1... | collective-permute-start | bytes 230408 | tf_op jit(solution)/shard_map/ppermute | solution.py:23
  58.5 1.2 collective-permute-done.5
  60.0 2.9 collective-permute-start.6
  62.9 1.9 collective-permute-start.7
  64.9 1.6 scatter_custom_fusion.1
  66.4 0.7 all_to_all.13
  67.2 12.0 %all-to-all-start.1 = ((s32[128,1,4]{2,1,0:T(1,128)}), s32[128,1,4]{2,1,0:T(1,128)S(1)}, u32[]{:S(2)}, u32[]{:S(2)}) async-start(s32[128,1,4]{2,1,0:T(1,128)} %bitcast.22), calls=%async_computation.1 | async-start | bytes 131072 | tf_op jit(solution)/shard_map/all_to_all | solution.py:101
  79.8 1.6 fusion.20
  81.4 3.3 collective-permute-start.8
  84.7 6.0 %collective-permute-start.9 = (bf16[3,100,1,128]{3,1,2,0:T(8,128)(2,1)S(1)}, bf16[3,100,1,128]{3,1,2,0:T(8,128)(2,1)S(1)}, u32[]{:S(2)}, u32[]{:S(2)}) collective-permute-start(bf16[3,100,1,128]{3,1,2,0:T(8,128)(2,1)S(1)} %get-tuple-element.41), channel_id=1, source_target_pairs={{1,0},{2,1},{3,2},{4,3},{5,4},{6,5},{7,6},{8,7},{9,8},{10,9},{11,1... | collective-permute-start | bytes 230408 | tf_op jit(solution)/shard_map/ppermute | solution.py:23
  90.9 1.3 collective-permute-done.9
  92.3 1.2 fusion.138
  93.5 8.6 %collective-permute-start.10 = (bf16[3,100,6,1]{3,1,2,0:T(8,128)(2,1)}, bf16[3,100,6,1]{3,1,2,0:T(8,128)(2,1)S(1)}, u32[]{:S(2)}, u32[]{:S(2)}) collective-permute-start(bf16[3,100,6,1]{3,1,2,0:T(8,128)(2,1)} %get-tuple-element.30), channel_id=1, source_target_pairs={{0,32},{32,64},{64,96},{1,33},{33,65},{65,97},{2,34},{34,66},{66,9... | collective-permute-start | bytes 10808 | tf_op jit(solution)/shard_map/ppermute | solution.py:21
  102.1 2.1 collective-permute-start.11
  104.6 7.1 %scatter_fusion = f32[512,3,100]{2,1,0:T(4,128)S(1)} fusion(f32[512,3,100]{2,1,0:T(4,128)S(1)} %broadcast_in_dim.33, s32[256]{0:T(256)S(1)} %bitcast.104, f32[256,3,100]{2,1,0:T(4,128)S(1)} %copy.45), kind=kCustom, calls=%fused_computation.2 | custom fusion | bytes 922624 | tf_op jit(solution)/shard_map/scatter | solution.py:97
  111.7 1.1 copy.47
  112.8 7.0 %collective-permute-done.11 = bf16[3,100,6,1]{3,1,2,0:T(8,128)(2,1)S(1)} collective-permute-done((bf16[3,100,6,1]{3,1,2,0:T(8,128)(2,1)}, bf16[3,100,6,1]{3,1,2,0:T(8,128)(2,1)S(1)}, u32[]{:S(2)}, u32[]{:S(2)}) %collective-permute-start.11) | collective-permute-done | bytes 3632 | tf_op jit(solution)/shard_map/ppermute | solution.py:23
  120.4 1.6 fusion.21
  122.0 2.4 collective-permute-start.12
  124.5 6.7 %collective-permute-start.13 = (bf16[3,100,1,128]{3,1,2,0:T(8,128)(2,1)S(1)}, bf16[3,100,1,128]{3,1,2,0:T(8,128)(2,1)S(1)}, u32[]{:S(2)}, u32[]{:S(2)}) collective-permute-start(bf16[3,100,1,128]{3,1,2,0:T(8,128)(2,1)S(1)} %get-tuple-element.39), channel_id=1, source_target_pairs={{1,0},{2,1},{3,2},{4,3},{5,4},{6,5},{7,6},{8,7},{9,8},{10,9},{11,1... | collective-permute-start | bytes 230408 | tf_op jit(solution)/shard_map/ppermute | solution.py:23
  131.2 8.4 %all-to-all-start = ((f32[128,4,3,100]{3,1,2,0:T(4,128)}), f32[128,4,3,100]{3,1,2,0:T(4,128)S(1)}, u32[]{:S(2)}, u32[]{:S(2)}) async-start(f32[128,4,3,100]{3,1,2,0:T(4,128)} %copy.47), calls=%async_computation | async-start | bytes 1572864 | tf_op jit(solution)/shard_map/all_to_all | solution.py:102
  140.2 7.7 %collective-permute-start.14 = (bf16[3,100,6,1]{3,1,2,0:T(8,128)(2,1)S(1)}, bf16[3,100,6,1]{3,1,2,0:T(8,128)(2,1)S(1)}, u32[]{:S(2)}, u32[]{:S(2)}) collective-permute-start(bf16[3,100,6,1]{3,1,2,0:T(8,128)(2,1)S(1)} %get-tuple-element.28), channel_id=1, source_target_pairs={{0,32},{32,64},{64,96},{1,33},{33,65},{65,97},{2,34},{34,66},{66,9... | collective-permute-start | bytes 10808 | tf_op jit(solution)/shard_map/ppermute | solution.py:21
  147.9 1.9 collective-permute-start.15
  150.1 13.9 %collective-permute-done.14 = bf16[3,100,6,1]{3,1,2,0:T(8,128)(2,1)S(1)} collective-permute-done((bf16[3,100,6,1]{3,1,2,0:T(8,128)(2,1)S(1)}, bf16[3,100,6,1]{3,1,2,0:T(8,128)(2,1)S(1)}, u32[]{:S(2)}, u32[]{:S(2)}) %collective-permute-start.14) | collective-permute-done | bytes 3632 | tf_op jit(solution)/shard_map/ppermute | solution.py:21
  164.0 0.8 copy-done.4
  164.7 9.6 %collective-permute-done.15 = bf16[3,100,6,1]{3,1,2,0:T(8,128)(2,1)} collective-permute-done((bf16[3,100,6,1]{3,1,2,0:T(8,128)(2,1)S(1)}, bf16[3,100,6,1]{3,1,2,0:T(8,128)(2,1)}, u32[]{:S(2)}, u32[]{:S(2)}) %collective-permute-start.15) | collective-permute-done | bytes 3632 | tf_op jit(solution)/shard_map/ppermute | solution.py:23
  174.4 1.7 maximum_convert_fusion.3
  176.1 1.6 fusion.22
  177.7 2.4 collective-permute-start.16
  180.1 6.8 %collective-permute-start.17 = (bf16[3,100,1,128]{3,1,2,0:T(8,128)(2,1)S(1)}, bf16[3,100,1,128]{3,1,2,0:T(8,128)(2,1)S(1)}, u32[]{:S(2)}, u32[]{:S(2)}) collective-permute-start(bf16[3,100,1,128]{3,1,2,0:T(8,128)(2,1)S(1)} %get-tuple-element.37), channel_id=1, source_target_pairs={{1,0},{2,1},{3,2},{4,3},{5,4},{6,5},{7,6},{8,7},{9,8},{10,9},{11,1... | collective-permute-start | bytes 230408 | tf_op jit(solution)/shard_map/ppermute | solution.py:23
  187.1 1.2 collective-permute-done.17
  188.6 2.8 collective-permute-start.18
  191.4 2.1 collective-permute-start.19
  193.8 3.2 collective-permute-done.18
  197.0 0.8 copy-done.3
  197.8 10.7 %collective-permute-done.19 = bf16[3,100,6,1]{3,1,2,0:T(8,128)(2,1)} collective-permute-done((bf16[3,100,6,1]{3,1,2,0:T(8,128)(2,1)S(1)}, bf16[3,100,6,1]{3,1,2,0:T(8,128)(2,1)}, u32[]{:S(2)}, u32[]{:S(2)}) %collective-permute-start.19) | collective-permute-done | bytes 3632 | tf_op jit(solution)/shard_map/ppermute | solution.py:23
  208.5 1.7 maximum_convert_fusion.4
  210.3 1.6 fusion.23
  212.6 2.1 gather_fusion
  214.6 1.8 convert_bitcast_fusion
  218.3 0.8 copy.56
  219.4 1.9 fusion.36
  221.6 1.5 fusion.94
  223.2 0.8 fusion.116
  224.4 10.7 %all-to-all-start.2 = ((f32[128,4,100]{2,1,0:T(4,128)}), f32[128,4,100]{2,1,0:T(4,128)S(1)}, u32[]{:S(2)}, u32[]{:S(2)}) async-start(f32[128,4,100]{2,1,0:T(4,128)} %bitcast.35), calls=%async_computation.2 | async-start | bytes 524288 | tf_op jit(solution)/shard_map/all_to_all | solution.py:125
  235.1 1.1 copy.60
  236.2 12.9 %all_gather.3 = bf16[8,100,512]{2,1,0:T(8,128)(2,1)S(1)} all-gather(bf16[2,100,512]{2,1,0:T(8,128)(2,1)S(1)} %copy.52), channel_id=1, replica_groups=mesh['mem'=4,'lat'=4,'lon'=32] {'mem'}, dimensions={0}, use_global_device_ids=true | all-gather | bytes 1024000 | tf_op jit(solution)/shard_map/all_gather | solution.py:130
  249.4 3.9 %fusion.33 = f32[8]{0:T(128)S(1)} fusion(f32[100,512,1]{1,2,0:T(1,128)S(1)} %copy.60, f32[8,100,512]{2,1,0:T(8,128)S(1)} %convert_multiply_fusion), kind=kOutput, calls=%fused_computation.37 | convolution fusion | flops 4915208 | bytes 1843232 | tf_op jit(solution)/shard_map/mks,ks->m/dot_general | solution.py:138
  253.2 2.6 fusion.27
  255.8 68.0 %all-reduce = (f32[8,8]{1,0:T(8,128)S(1)}, f32[8]{0:T(128)S(1)}) all-reduce(f32[8,8]{1,0:T(8,128)S(1)} %fusion.27, f32[8]{0:T(128)S(1)} %fusion.33), channel_id=1, replica_groups=mesh['mem'=4,'lat'=4,'lon'=32] {'lon'}, use_global_device_ids=true, to_apply=%region_5.6 | all-reduce | flops 72 | bytes 576 | tf_op jit(solution)/shard_map/psum | solution.py:10
  323.8 25.4 %all-reduce.1 = (f32[8,8]{1,0:T(8,128)}, f32[8]{0:T(128)}) all-reduce(f32[8,8]{1,0:T(8,128)S(1)} %get-tuple-element.20, f32[8]{0:T(128)S(1)} %get-tuple-element.21), channel_id=1, replica_groups=mesh['mem'=4,'lat'=4,'lon'=32] {'lat'}, use_global_device_ids=true, to_apply=%region_6.7 | all-reduce | flops 72 | bytes 576 | tf_op jit(solution)/shard_map/psum | solution.py:10
  350.1 0.7 copy.58
  (95 shorter events, 10.2 us)
Async XLA Ops:
  0.6 18.6 %copy-start = (f32[16,100]{1,0:T(8,128)S(1)}, f32[16,100]{1,0:T(8,128)}, u32[]{:S(2)}) copy-start(f32[16,100]{1,0:T(8,128)} %param.14) | copy-start | bytes 19204
  1.6 19.1 %collective-permute-start.1 = (bf16[3,100,1,128]{3,1,2,0:T(8,128)(2,1)S(1)}, bf16[3,100,1,128]{3,1,2,0:T(8,128)(2,1)S(1)}, u32[]{:S(2)}, u32[]{:S(2)}) collective-permute-start(bf16[3,100,1,128]{3,1,2,0:T(8,128)(2,1)S(1)} %broadcast_in_dim.30), channel_id=1, source_target_pairs={{1,0},{2,1},{3,2},{4,3},{5,4},{6,5},{7,6},{8,7},{9,8},{10,9},{11,1... | collective-permute-start | bytes 230408 | tf_op jit(solution)/shard_map/ppermute | solution.py:23
  16.2 9.1 %collective-permute-start = (bf16[3,100,1,128]{3,1,2,0:T(8,128)(2,1)S(1)}, bf16[3,100,1,128]{3,1,2,0:T(8,128)(2,1)S(1)}, u32[]{:S(2)}, u32[]{:S(2)}) collective-permute-start(bf16[3,100,1,128]{3,1,2,0:T(8,128)(2,1)S(1)} %broadcast_in_dim.28), channel_id=1, source_target_pairs={{0,1},{1,2},{2,3},{3,4},{4,5},{5,6},{6,7},{7,8},{8,9},{9,10},{10,1... | collective-permute-start | bytes 230408 | tf_op jit(solution)/shard_map/ppermute | solution.py:21
  18.9 15.4 %copy-start.10 = (s32[4,128]{1,0:T(4,128)S(1)}, s32[4,128]{1,0:T(4,128)}, u32[]{:S(2)}) copy-start(s32[4,128]{1,0:T(4,128)} %param.13) | copy-start | bytes 6148
  18.9 15.4 %copy-start.8 = (bf16[2,100,100]{2,0,1:T(2,128)(2,1)S(1)}, bf16[2,100,100]{2,0,1:T(2,128)(2,1)}, u32[]{:S(2)}) copy-start(bf16[2,100,100]{2,0,1:T(2,128)(2,1)} %param.17) | copy-start | bytes 120004
  25.6 21.9 %copy-start.11 = (bf16[100,100]{1,0:T(8,128)(2,1)S(1)}, bf16[100,100]{1,0:T(8,128)(2,1)}, u32[]{:S(2)}) copy-start(bf16[100,100]{1,0:T(8,128)(2,1)} %param.18) | copy-start | bytes 60004
  25.6 12.5 %collective-permute-start.2 = (bf16[3,100,6,1]{3,1,2,0:T(8,128)(2,1)S(1)}, bf16[3,100,6,1]{3,1,2,0:T(8,128)(2,1)S(1)}, u32[]{:S(2)}, u32[]{:S(2)}) collective-permute-start(bf16[3,100,6,1]{3,1,2,0:T(8,128)(2,1)S(1)} %get-tuple-element.34), channel_id=1, source_target_pairs={{0,32},{32,64},{64,96},{1,33},{33,65},{65,97},{2,34},{34,66},{66,9... | collective-permute-start | bytes 10808 | tf_op jit(solution)/shard_map/ppermute | solution.py:21
  32.3 14.5 %collective-permute-start.3 = (bf16[3,100,6,1]{3,1,2,0:T(8,128)(2,1)S(1)}, bf16[3,100,6,1]{3,1,2,0:T(8,128)(2,1)S(1)}, u32[]{:S(2)}, u32[]{:S(2)}) collective-permute-start(bf16[3,100,6,1]{3,1,2,0:T(8,128)(2,1)S(1)} %get-tuple-element.35), channel_id=1, source_target_pairs={{32,0},{64,32},{96,64},{33,1},{65,33},{97,65},{34,2},{66,34},{98,6... | collective-permute-start | bytes 10808 | tf_op jit(solution)/shard_map/ppermute | solution.py:23
  47.5 10.8 %copy-start.9 = (s32[256,1]{0,1:T(1,128)S(1)}, s32[256,1]{0,1:T(1,128)}, u32[]{:S(2)}) copy-start(s32[256,1]{0,1:T(1,128)} %param.19) | copy-start | bytes 3076
  49.1 9.4 %collective-permute-start.4 = (bf16[3,100,1,128]{3,1,2,0:T(8,128)(2,1)S(1)}, bf16[3,100,1,128]{3,1,2,0:T(8,128)(2,1)S(1)}, u32[]{:S(2)}, u32[]{:S(2)}) collective-permute-start(bf16[3,100,1,128]{3,1,2,0:T(8,128)(2,1)S(1)} %get-tuple-element.42), channel_id=1, source_target_pairs={{0,1},{1,2},{2,3},{3,4},{4,5},{5,6},{6,7},{7,8},{8,9},{9,10},{10,1... | collective-permute-start | bytes 230408 | tf_op jit(solution)/shard_map/ppermute | solution.py:21
  51.0 8.7 %collective-permute-start.5 = (bf16[3,100,1,128]{3,1,2,0:T(8,128)(2,1)S(1)}, bf16[3,100,1,128]{3,1,2,0:T(8,128)(2,1)S(1)}, u32[]{:S(2)}, u32[]{:S(2)}) collective-permute-start(bf16[3,100,1,128]{3,1,2,0:T(8,128)(2,1)S(1)} %get-tuple-element.43), channel_id=1, source_target_pairs={{1,0},{2,1},{3,2},{4,3},{5,4},{6,5},{7,6},{8,7},{9,8},{10,9},{11,1... | collective-permute-start | bytes 230408 | tf_op jit(solution)/shard_map/ppermute | solution.py:23
  60.0 19.2 %collective-permute-start.6 = (bf16[3,100,6,1]{3,1,2,0:T(8,128)(2,1)S(1)}, bf16[3,100,6,1]{3,1,2,0:T(8,128)(2,1)S(1)}, u32[]{:S(2)}, u32[]{:S(2)}) collective-permute-start(bf16[3,100,6,1]{3,1,2,0:T(8,128)(2,1)S(1)} %get-tuple-element.32), channel_id=1, source_target_pairs={{0,32},{32,64},{64,96},{1,33},{33,65},{65,97},{2,34},{34,66},{66,9... | collective-permute-start | bytes 10808 | tf_op jit(solution)/shard_map/ppermute | solution.py:21
  62.9 16.3 %collective-permute-start.7 = (bf16[3,100,6,1]{3,1,2,0:T(8,128)(2,1)S(1)}, bf16[3,100,6,1]{3,1,2,0:T(8,128)(2,1)S(1)}, u32[]{:S(2)}, u32[]{:S(2)}) collective-permute-start(bf16[3,100,6,1]{3,1,2,0:T(8,128)(2,1)S(1)} %get-tuple-element.33), channel_id=1, source_target_pairs={{32,0},{64,32},{96,64},{33,1},{65,33},{97,65},{34,2},{66,34},{98,6... | collective-permute-start | bytes 10808 | tf_op jit(solution)/shard_map/ppermute | solution.py:23
  67.2 64.1 %all-to-all-start.1 = ((s32[128,1,4]{2,1,0:T(1,128)}), s32[128,1,4]{2,1,0:T(1,128)S(1)}, u32[]{:S(2)}, u32[]{:S(2)}) async-start(s32[128,1,4]{2,1,0:T(1,128)} %bitcast.22), calls=%async_computation.1 | async-start | bytes 131072 | tf_op jit(solution)/shard_map/all_to_all | solution.py:101
  79.8 11.0 %copy-start.5 = (f32[256,100]{0,1:T(8,128)S(1)}, f32[256,100]{0,1:T(8,128)}, u32[]{:S(2)}) copy-start(f32[256,100]{0,1:T(8,128)} %param.23) | copy-start | bytes 307204
  79.8 11.0 %copy-start.6 = (f32[256,100]{0,1:T(8,128)S(1)}, f32[256,100]{0,1:T(8,128)}, u32[]{:S(2)}) copy-start(f32[256,100]{0,1:T(8,128)} %param.22) | copy-start | bytes 307204
  79.8 11.0 %copy-start.7 = (f32[256,100]{0,1:T(8,128)S(1)}, f32[256,100]{0,1:T(8,128)}, u32[]{:S(2)}) copy-start(f32[256,100]{0,1:T(8,128)} %param.21) | copy-start | bytes 307204
  81.4 9.5 %collective-permute-start.8 = (bf16[3,100,1,128]{3,1,2,0:T(8,128)(2,1)S(1)}, bf16[3,100,1,128]{3,1,2,0:T(8,128)(2,1)S(1)}, u32[]{:S(2)}, u32[]{:S(2)}) collective-permute-start(bf16[3,100,1,128]{3,1,2,0:T(8,128)(2,1)S(1)} %get-tuple-element.40), channel_id=1, source_target_pairs={{0,1},{1,2},{2,3},{3,4},{4,5},{5,6},{6,7},{7,8},{8,9},{9,10},{10,1... | collective-permute-start | bytes 230408 | tf_op jit(solution)/shard_map/ppermute | solution.py:21
  84.7 7.5 %collective-permute-start.9 = (bf16[3,100,1,128]{3,1,2,0:T(8,128)(2,1)S(1)}, bf16[3,100,1,128]{3,1,2,0:T(8,128)(2,1)S(1)}, u32[]{:S(2)}, u32[]{:S(2)}) collective-permute-start(bf16[3,100,1,128]{3,1,2,0:T(8,128)(2,1)S(1)} %get-tuple-element.41), channel_id=1, source_target_pairs={{1,0},{2,1},{3,2},{4,3},{5,4},{6,5},{7,6},{8,7},{9,8},{10,9},{11,1... | collective-permute-start | bytes 230408 | tf_op jit(solution)/shard_map/ppermute | solution.py:23
  93.5 19.3 %collective-permute-start.10 = (bf16[3,100,6,1]{3,1,2,0:T(8,128)(2,1)}, bf16[3,100,6,1]{3,1,2,0:T(8,128)(2,1)S(1)}, u32[]{:S(2)}, u32[]{:S(2)}) collective-permute-start(bf16[3,100,6,1]{3,1,2,0:T(8,128)(2,1)} %get-tuple-element.30), channel_id=1, source_target_pairs={{0,32},{32,64},{64,96},{1,33},{33,65},{65,97},{2,34},{34,66},{66,9... | collective-permute-start | bytes 10808 | tf_op jit(solution)/shard_map/ppermute | solution.py:21
  102.1 17.7 %collective-permute-start.11 = (bf16[3,100,6,1]{3,1,2,0:T(8,128)(2,1)}, bf16[3,100,6,1]{3,1,2,0:T(8,128)(2,1)S(1)}, u32[]{:S(2)}, u32[]{:S(2)}) collective-permute-start(bf16[3,100,6,1]{3,1,2,0:T(8,128)(2,1)} %get-tuple-element.31), channel_id=1, source_target_pairs={{32,0},{64,32},{96,64},{33,1},{65,33},{97,65},{34,2},{66,34},{98,6... | collective-permute-start | bytes 10808 | tf_op jit(solution)/shard_map/ppermute | solution.py:23
  122.0 17.9 %collective-permute-start.12 = (bf16[3,100,1,128]{3,1,2,0:T(8,128)(2,1)S(1)}, bf16[3,100,1,128]{3,1,2,0:T(8,128)(2,1)S(1)}, u32[]{:S(2)}, u32[]{:S(2)}) collective-permute-start(bf16[3,100,1,128]{3,1,2,0:T(8,128)(2,1)S(1)} %get-tuple-element.38), channel_id=1, source_target_pairs={{0,1},{1,2},{2,3},{3,4},{4,5},{5,6},{6,7},{7,8},{8,9},{9,10},{10,1... | collective-permute-start | bytes 230408 | tf_op jit(solution)/shard_map/ppermute | solution.py:21
  124.5 15.4 %collective-permute-start.13 = (bf16[3,100,1,128]{3,1,2,0:T(8,128)(2,1)S(1)}, bf16[3,100,1,128]{3,1,2,0:T(8,128)(2,1)S(1)}, u32[]{:S(2)}, u32[]{:S(2)}) collective-permute-start(bf16[3,100,1,128]{3,1,2,0:T(8,128)(2,1)S(1)} %get-tuple-element.39), channel_id=1, source_target_pairs={{1,0},{2,1},{3,2},{4,3},{5,4},{6,5},{7,6},{8,7},{9,8},{10,9},{11,1... | collective-permute-start | bytes 230408 | tf_op jit(solution)/shard_map/ppermute | solution.py:23
  131.2 87.9 %all-to-all-start = ((f32[128,4,3,100]{3,1,2,0:T(4,128)}), f32[128,4,3,100]{3,1,2,0:T(4,128)S(1)}, u32[]{:S(2)}, u32[]{:S(2)}) async-start(f32[128,4,3,100]{3,1,2,0:T(4,128)} %copy.47), calls=%async_computation | async-start | bytes 1572864 | tf_op jit(solution)/shard_map/all_to_all | solution.py:102
  140.2 23.8 %collective-permute-start.14 = (bf16[3,100,6,1]{3,1,2,0:T(8,128)(2,1)S(1)}, bf16[3,100,6,1]{3,1,2,0:T(8,128)(2,1)S(1)}, u32[]{:S(2)}, u32[]{:S(2)}) collective-permute-start(bf16[3,100,6,1]{3,1,2,0:T(8,128)(2,1)S(1)} %get-tuple-element.28), channel_id=1, source_target_pairs={{0,32},{32,64},{64,96},{1,33},{33,65},{65,97},{2,34},{34,66},{66,9... | collective-permute-start | bytes 10808 | tf_op jit(solution)/shard_map/ppermute | solution.py:21
  147.9 26.5 %collective-permute-start.15 = (bf16[3,100,6,1]{3,1,2,0:T(8,128)(2,1)S(1)}, bf16[3,100,6,1]{3,1,2,0:T(8,128)(2,1)}, u32[]{:S(2)}, u32[]{:S(2)}) collective-permute-start(bf16[3,100,6,1]{3,1,2,0:T(8,128)(2,1)S(1)} %get-tuple-element.29), channel_id=1, source_target_pairs={{32,0},{64,32},{96,64},{33,1},{65,33},{97,65},{34,2},{66,34},{98,6... | collective-permute-start | bytes 10808 | tf_op jit(solution)/shard_map/ppermute | solution.py:23
  164.0 0.8 copy-start.4
  177.7 9.4 %collective-permute-start.16 = (bf16[3,100,1,128]{3,1,2,0:T(8,128)(2,1)S(1)}, bf16[3,100,1,128]{3,1,2,0:T(8,128)(2,1)S(1)}, u32[]{:S(2)}, u32[]{:S(2)}) collective-permute-start(bf16[3,100,1,128]{3,1,2,0:T(8,128)(2,1)S(1)} %get-tuple-element.36), channel_id=1, source_target_pairs={{0,1},{1,2},{2,3},{3,4},{4,5},{5,6},{6,7},{7,8},{8,9},{9,10},{10,1... | collective-permute-start | bytes 230408 | tf_op jit(solution)/shard_map/ppermute | solution.py:21
  180.1 8.2 %collective-permute-start.17 = (bf16[3,100,1,128]{3,1,2,0:T(8,128)(2,1)S(1)}, bf16[3,100,1,128]{3,1,2,0:T(8,128)(2,1)S(1)}, u32[]{:S(2)}, u32[]{:S(2)}) collective-permute-start(bf16[3,100,1,128]{3,1,2,0:T(8,128)(2,1)S(1)} %get-tuple-element.37), channel_id=1, source_target_pairs={{1,0},{2,1},{3,2},{4,3},{5,4},{6,5},{7,6},{8,7},{9,8},{10,9},{11,1... | collective-permute-start | bytes 230408 | tf_op jit(solution)/shard_map/ppermute | solution.py:23
  188.6 8.4 %collective-permute-start.18 = (bf16[3,100,6,1]{3,1,2,0:T(8,128)(2,1)S(1)}, bf16[3,100,6,1]{3,1,2,0:T(8,128)(2,1)S(1)}, u32[]{:S(2)}, u32[]{:S(2)}) collective-permute-start(bf16[3,100,6,1]{3,1,2,0:T(8,128)(2,1)S(1)} %get-tuple-element.26), channel_id=1, source_target_pairs={{0,32},{32,64},{64,96},{1,33},{33,65},{65,97},{2,34},{34,66},{66,9... | collective-permute-start | bytes 10808 | tf_op jit(solution)/shard_map/ppermute | solution.py:21
  191.4 17.1 %collective-permute-start.19 = (bf16[3,100,6,1]{3,1,2,0:T(8,128)(2,1)S(1)}, bf16[3,100,6,1]{3,1,2,0:T(8,128)(2,1)}, u32[]{:S(2)}, u32[]{:S(2)}) collective-permute-start(bf16[3,100,6,1]{3,1,2,0:T(8,128)(2,1)S(1)} %get-tuple-element.27), channel_id=1, source_target_pairs={{32,0},{64,32},{96,64},{33,1},{65,33},{97,65},{34,2},{66,34},{98,6... | collective-permute-start | bytes 10808 | tf_op jit(solution)/shard_map/ppermute | solution.py:23
  197.0 0.8 copy-start.3
  211.8 0.7 copy-start.1
  216.4 1.2 copy-start.2
  216.4 1.9 slice-start
  224.4 124.9 %all-to-all-start.2 = ((f32[128,4,100]{2,1,0:T(4,128)}), f32[128,4,100]{2,1,0:T(4,128)S(1)}, u32[]{:S(2)}, u32[]{:S(2)}) async-start(f32[128,4,100]{2,1,0:T(4,128)} %bitcast.35), calls=%async_computation.2 | async-start | bytes 524288 | tf_op jit(solution)/shard_map/all_to_all | solution.py:125
